TPU v7x, 256 devices: a whole 4x4x8 slice. The times are simulated.
256 devices in a mesh: member: 2 (over y_lo), lat: 4 (over x), lon: 32 (over z, y_hi, core).
Axes of the slice: x: 4, y: 4 (y_hi: 2, y_lo: 2; y = y_hi * 2 + y_lo), z: 8, core: 2. Of those that a mesh axis runs over, the one named last changes fastest.
Arguments:
- features: bfloat16 [2, 720, 1440, 128], P('member', 'lat', 'lon'), may hold values from -6 to 6
- present_condition: bfloat16 [2, 720, 1440, 80], P('member', 'lat', 'lon'), may hold values from -6 to 6
- target: bfloat16 [720, 1440, 80], P('lat', 'lon'), may hold values from -8 to 8
- filter_weights_tensor: bfloat16 [3, 3, 128, 80], replicated, may hold values from -0.1875 to 0.1875
Outputs:
- predicted_outputs: bfloat16 [2, 720, 1440, 80], P('member', 'lat', 'lon')
- objective_mean: float32 [], replicated
- hidden_state_slope: bfloat16 [2, 720, 1440, 128], P('member', 'lat', 'lon')
- filter_weights_slope: float32 [3, 3, 128, 80], replicated
All inputs are finite; a program needn't handle non-finite values.
Results may differ from a plain program's by a relative error of at most 0.0095.
Values may be sent and summed in bfloat16 or wider, within the bound.
No kernel may reach another device: no remote copies, remote signals or barrier semaphores. Data moves between devices by JAX's collectives and lax.ppermute only.
A program may use at most 128 MiB of HBM per device.

v0:
```python
import math
import jax
import jax.numpy as jnp
from jax import lax
from jax.sharding import PartitionSpec as P

epsilon = 1e-06


def padded(block, sides, width, periodic):
    for axis, dim in sides:
        count = lax.axis_size(axis)
        forward = [(i, i + 1) for i in range(count - 1)]
        if periodic:
            forward.append((count - 1, 0))
        backward = [(target, source) for source, target in forward]
        low = lax.ppermute(
            lax.slice_in_dim(block, block.shape[dim] - width, None, axis=dim), axis, forward
        )
        high = lax.ppermute(lax.slice_in_dim(block, 0, width, axis=dim), axis, backward)
        block = jnp.concatenate([low, block, high], axis=dim)
    return block


def partner(value, axis, distance):
    mask = 2**distance
    pairs = [(source, source ^ mask) for source in range(lax.axis_size(axis))]
    return lax.ppermute(value, axis, pairs)


def stencil_filter_step(haloed_grid_array, weights_hwio):
    result = lax.conv_general_dilated(
        haloed_grid_array[None],
        weights_hwio,
        (1, 1),
        "VALID",
        dimension_numbers=("NHWC", "HWIO", "NHWC"),
        preferred_element_type=jnp.float32,
    )
    return result[0]


def latitude_weights(row_index, total_rows):
    scale = math.pi / total_rows
    angles = 0.5 * math.pi - (row_index.astype(jnp.float32) + 0.5) * scale
    every_row = (
        0.5 * math.pi - (jnp.arange(total_rows, dtype=jnp.int32).astype(jnp.float32) + 0.5) * scale
    )
    return jnp.cos(angles) / jnp.mean(jnp.cos(every_row))


def tap_products(haloed_grid_array, cotangent):
    lat_rows, lon_cols, channels = cotangent.shape
    inputs = haloed_grid_array.shape[2]
    flat_grad = cotangent.reshape(lat_rows * lon_cols, channels)
    stacked = []
    for row_tap in range(3):
        across = []
        for col_tap in range(3):
            window = haloed_grid_array[
                row_tap : row_tap + lat_rows, col_tap : col_tap + lon_cols
            ].reshape(lat_rows * lon_cols, inputs)
            across.append(
                lax.dot_general(
                    window, flat_grad, (((0,), (0,)), ((), ())), preferred_element_type=jnp.float32
                )
            )
        stacked.append(jnp.stack(across))
    return jnp.stack(stacked)


def extend_features(field):
    widened = padded(field, (("lon", 1),), 1, True)
    return padded(widened, (("lat", 0),), 1, False)


def extend_cotangent(field):
    widened = padded(field, (("lon", 1),), 1, True)
    return padded(widened, (("lat", 0),), 1, False)


def local(features, present_condition, target, filter_weights_tensor):
    lat_rows = features.shape[1]
    lon_cols = features.shape[2]
    total_rows = lat_rows * lax.axis_size("lat")
    total_cols = lon_cols * lax.axis_size("lon")
    haloed_grid_array = extend_features(features[0])
    predicted_outputs = (
        present_condition[0].astype(jnp.float32)
        + stencil_filter_step(haloed_grid_array, filter_weights_tensor)
    ).astype(jnp.bfloat16)
    companion_sample = partner(predicted_outputs, "member", 0)
    truth = target.astype(jnp.float32)
    energy_metrics = predicted_outputs.astype(jnp.float32)
    misfit = energy_metrics - truth
    errors = jnp.sqrt(jnp.sum(misfit * misfit, axis=-1) + epsilon)
    spread = energy_metrics - companion_sample.astype(jnp.float32)
    pair = jnp.sqrt(jnp.sum(spread * spread, axis=-1) + epsilon)
    row_index = lax.axis_index("lat") * lat_rows + jnp.arange(lat_rows, dtype=jnp.int32)
    weights = latitude_weights(row_index, total_rows)[:, None]
    local_total = jnp.sum(weights * (0.5 * errors - 0.25 * pair))
    cotangent = (
        weights[..., None] * (0.5 * misfit / errors[..., None] - 0.5 * spread / pair[..., None])
    ).astype(jnp.bfloat16)
    flipped = jnp.transpose(filter_weights_tensor[::-1, ::-1], (0, 1, 3, 2))
    hidden_state_slope = stencil_filter_step(extend_cotangent(cotangent), flipped).astype(
        jnp.bfloat16
    )
    partial_grad = tap_products(haloed_grid_array, cotangent)
    summed_grad, total = lax.psum((partial_grad, local_total), ("member", "lat", "lon"))
    objective_mean = total / (total_rows * total_cols)
    filter_weights_slope = summed_grad / math.sqrt(2.0 * total_rows * total_cols)
    return (predicted_outputs[None], objective_mean, hidden_state_slope[None], filter_weights_slope)


def solution(mesh):
    in_specs = (
        P("member", "lat", "lon", None),
        P("member", "lat", "lon", None),
        P("lat", "lon", None),
        P(),
    )
    out_specs = (P("member", "lat", "lon", None), P(), P("member", "lat", "lon", None), P())
    return jax.shard_map(local, mesh=mesh, in_specs=in_specs, out_specs=out_specs, check_vma=False)
```

profile of v0, /device:TPU:1, one launch (start us, length us, event | category | flops | bytes accessed | tf_op | source)
XLA Modules:
  0.0 395.3 jit_solution(8616252345672613163)
XLA Ops:
  7.2 1.0 fusion.76
  8.2 4.4 %collective-permute-start = (bf16[180,1,128]{2,0,1:T(8,128)(2,1)S(1)}, bf16[180,1,128]{2,0,1:T(8,128)(2,1)S(1)}, u32[]{:S(2)}, u32[]{:S(2)}) collective-permute-start(bf16[180,1,128]{2,0,1:T(8,128)(2,1)S(1)} %get-tuple-element.10), channel_id=1, source_target_pairs={{0,1},{1,2},{2,3},{3,4},{4,5},{5,6},{6,7},{7,8},{8,9},{9,10},{10,1... | collective-permute-start | bytes 138248 | tf_op jit(solution)/shard_map/ppermute | solution.py:17
  12.6 1.2 collective-permute-done
  13.7 3.8 collective-permute-done.1
  17.6 1.0 pad_maximum_fusion.5
  18.6 3.1 collective-permute-start.2
  21.7 1.3 collective-permute-start.3
  23.0 3.3 collective-permute-done.3
  26.3 1.0 maximum_bitcast_fusion
  28.3 6.8 %broadcast_select_fusion = f32[180,8,6,80]{3,1,2,0:T(8,128)} fusion(pred[8,6]{0,1:T(8,128)(4,1)S(1)} %copy-done.10, bf16[3,3,128,80]{2,3,1,0:T(8,128)(2,1)S(1)} %copy-done, bf16[182,1,7,2,128]{4,2,3,0,1:T(8,128)(2,1)S(1)} %slice.78, bf16[182,1,8,6,128]{4,2,3,0,1:T(8,128)(2,1)S(1)} %copy.17), kind=kOutput, calls=%fused_computation.28 | convolution fusion | flops 1602161664 | bytes 5837872 | tf_op jit(solution)/shard_map/conv_general_dilated | solution.py:32
  35.1 6.2 %copy.18 = f32[180,8,6,80]{0,3,2,1:T(8,128)} copy(f32[180,8,6,80]{3,1,2,0:T(8,128)} %broadcast_select_fusion) | data formatting | bytes 5529600 | tf_op jit(solution)/shard_map/conv_general_dilated | solution.py:32
  41.3 4.4 %fusion.3 = bf16[1,180,45,80]{1,3,2,0:T(8,128)(2,1)} fusion(f32[180,1,48,80]{0,3,2,1:T(8,128)} %bitcast.83, bf16[1,180,45,80]{1,3,2,0:T(8,128)(2,1)} %param.5), kind=kLoop, calls=%fused_computation.9 | loop fusion | flops 1944000 | bytes 5184000 | tf_op jit(solution)/shard_map/convert_element_type | solution.py:91
  46.1 1.7 copy.27
  47.8 4.2 %reshape_squeeze.3 = bf16[8100,128]{1,0:T(8,128)(2,1)} reshape(bf16[1,180,45,128]{3,2,1,0:T(8,128)(2,1)} %copy.27) | data formatting | bytes 4147200 | tf_op jit(solution)/shard_map/reshape;squeeze | solution.py:62
  52.0 0.6 cosine_reduce_fusion
  53.4 4.4 %maximum_maximum_fusion = (bf16[181,47,128]{2,0,1:T(8,128)(2,1)}, bf16[181,47,128]{2,0,1:T(8,128)(2,1)}) fusion(bf16[180,1,128]{2,0,1:T(8,128)(2,1)S(1)} %collective-permute-done.1, bf16[180,45,128]{2,0,1:T(8,128)(2,1)S(1)} %bitcast.80, bf16[180,1,128]{2,0,1:T(8,128)(2,1)S(1)} %collective-permute-done, bf16[1,47,128]{2,0,1:T(2,128)(2,1)S(1)} %collective-permute-done.2, ...), kind=kLoop, calls=%fused_computation.26 | loop fusion | flops 17422336 | bytes 6545408 | tf_op jit(solution)/shard_map/concatenate | solution.py:21
  57.8 26.6 %collective-permute-done.4 = bf16[180,45,80]{0,2,1:T(8,128)(2,1)} collective-permute-done((bf16[180,45,80]{0,2,1:T(8,128)(2,1)}, bf16[180,45,80]{0,2,1:T(8,128)(2,1)}, u32[]{:S(2)}, u32[]{:S(2)}) %collective-permute-start.4) | collective-permute-done | bytes 1296032 | tf_op jit(solution)/shard_map/ppermute | solution.py:28
  84.3 3.6 multiply_reduce_fusion
  87.9 0.6 add_sqrt_fusion.1
  88.6 4.8 %multiply_convert_fusion = bf16[180,45,80]{0,2,1:T(8,128)(2,1)} fusion(bf16[180,45,80]{0,2,1:T(8,128)(2,1)S(1)} %copy-done.5, bf16[180,45,80]{0,2,1:T(8,128)(2,1)} %collective-permute-done.4, f32[180,45]{0,1:T(8,128)S(1)} %get-tuple-element.18, f32[180,45]{0,1:T(8,128)S(1)} %get-tuple-element.16, f32[180]{0:T(256)S(1)} %cosine_divide_fusion, ...), kind=kLoop, calls=%fused_computation.10 | loop fusion | flops 7776000 | bytes 5249520 | tf_op jit(solution)/shard_map/convert_element_type | solution.py:104
  93.4 4.7 %copy.26 = bf16[180,45,80]{2,1,0:T(8,128)(2,1)} copy(bf16[180,45,80]{0,2,1:T(8,128)(2,1)} %multiply_convert_fusion) | data formatting | bytes 2592000 | tf_op jit(solution)/shard_map/convert_element_type | solution.py:104
  98.1 3.0 fusion.44
  101.5 0.8 fusion.47
  102.2 0.8 fusion.50
  103.0 0.8 copy-done.6
  103.9 1.3 fusion.53
  105.1 1.3 fusion.56
  106.4 1.3 fusion.59
  107.7 4.3 %reshape.50 = bf16[8100,80]{1,0:T(8,128)(2,1)} reshape(bf16[180,45,80]{2,1,0:T(8,128)(2,1)} %copy.26) | data formatting | bytes 2592000 | tf_op jit(solution)/shard_map/reshape | solution.py:55
  112.0 5.5 %collective-permute-start.5 = (bf16[180,1,80]{0,2,1:T(8,128)(2,1)S(1)}, bf16[180,1,80]{0,2,1:T(8,128)(2,1)S(1)}, u32[]{:S(2)}, u32[]{:S(2)}) collective-permute-start(bf16[180,1,80]{0,2,1:T(8,128)(2,1)S(1)} %get-tuple-element.14), channel_id=1, source_target_pairs={{0,1},{1,2},{2,3},{3,4},{4,5},{5,6},{6,7},{7,8},{8,9},{9,10},{10,1... | collective-permute-start | bytes 86408 | tf_op jit(solution)/shard_map/ppermute | solution.py:17
  117.5 2.9 convolution_bitcast_fusion
  120.4 0.8 fusion.62
  121.2 0.8 fusion.65
  122.4 0.6 copy-done.8
  123.4 1.4 fusion.77
  124.8 1.6 copy.19
  126.4 3.2 collective-permute-start.7
  130.1 1.3 collective-permute-start.8
  131.4 0.8 pad_maximum_fusion.2
  132.2 81.6 %psum.14 = f32[]{:T(128)} all-reduce(f32[]{:T(128)} %get-tuple-element.17), channel_id=1, replica_groups=mesh['member'=2,'lat'=4,'lon'=32] {'member','lat','lon'}, use_global_device_ids=true, to_apply=%region_4.0 | all-reduce | flops 1 | bytes 8 | tf_op jit(solution)/shard_map/psum | solution.py:110
  215.0 1.4 copy.22
  216.3 2.4 maximum_bitcast_fusion.1
  219.1 3.4 copy.24
  222.5 1.3 slice.84
  223.8 7.1 %select_convert_fusion = bf16[180,8,6,128]{3,1,2,0:T(8,128)(2,1)S(1)} fusion(pred[8,6]{0,1:T(8,128)(4,1)S(1)} %copy-done.11, bf16[3,3,128,80]{2,3,1,0:T(8,128)(2,1)S(1)} %copy-done, bf16[182,1,7,2,80]{4,2,3,0,1:T(8,128)(2,1)S(1)} %slice.84, bf16[182,1,8,6,80]{4,2,3,0,1:T(8,128)(2,1)} %copy.24), kind=kOutput, calls=%fused_computation.6 | convolution fusion | flops 1600327680 | bytes 4201648 | tf_op jit(solution)/shard_map/conv_general_dilated | solution.py:32
  231.6 1.5 slice_bitcast_fusion.1
  233.1 152.1 %all-reduce.2.cloned.1.call-done = f32[3,3,128,80]{2,3,1,0:T(8,128)} async-done(((f32[3,3,128,80]{2,3,1,0:T(8,128)}), f32[3,3,128,80]{2,3,1,0:T(8,128)}) %all-reduce.2.cloned.1.call-update) | async-done | bytes 368656 | tf_op jit(solution)/shard_map/psum | solution.py:110
  385.2 1.8 broadcast_multiply_fusion
  (44 shorter events, 4.4 us)
Async XLA Ops:
  7.2 21.1 %copy-start = (bf16[3,3,128,80]{2,3,1,0:T(8,128)(2,1)S(1)}, bf16[3,3,128,80]{2,3,1,0:T(8,128)(2,1)}, u32[]{:S(2)}) copy-start(bf16[3,3,128,80]{2,3,1,0:T(8,128)(2,1)} %param.7) | copy-start | bytes 552964
  7.2 19.1 %copy-start.1 = (bf16[1,180,45,128]{3,1,2,0:T(8,128)(2,1)S(1)}, bf16[1,180,45,128]{3,1,2,0:T(8,128)(2,1)}, u32[]{:S(2)}) copy-start(bf16[1,180,45,128]{3,1,2,0:T(8,128)(2,1)} %param.4) | copy-start | bytes 6220804
  7.2 378.0 %all-reduce.2.cloned.1.call-start = ((), (), s32[]{:S(2)}) async-start(), calls=%async_computation | async-start | bytes 737280 | tf_op jit(solution)/shard_map/psum | solution.py:110
  8.2 5.5 %collective-permute-start = (bf16[180,1,128]{2,0,1:T(8,128)(2,1)S(1)}, bf16[180,1,128]{2,0,1:T(8,128)(2,1)S(1)}, u32[]{:S(2)}, u32[]{:S(2)}) collective-permute-start(bf16[180,1,128]{2,0,1:T(8,128)(2,1)S(1)} %get-tuple-element.10), channel_id=1, source_target_pairs={{0,1},{1,2},{2,3},{3,4},{4,5},{5,6},{6,7},{7,8},{8,9},{9,10},{10,1... | collective-permute-start | bytes 138248 | tf_op jit(solution)/shard_map/ppermute | solution.py:17
  12.6 5.0 %collective-permute-start.1 = (bf16[180,1,128]{2,0,1:T(8,128)(2,1)S(1)}, bf16[180,1,128]{2,0,1:T(8,128)(2,1)S(1)}, u32[]{:S(2)}, u32[]{:S(2)}) collective-permute-start(bf16[180,1,128]{2,0,1:T(8,128)(2,1)S(1)} %get-tuple-element.11), channel_id=1, source_target_pairs={{1,0},{2,1},{3,2},{4,3},{5,4},{6,5},{7,6},{8,7},{9,8},{10,9},{11,1... | collective-permute-start | bytes 138248 | tf_op jit(solution)/shard_map/ppermute | solution.py:20
  18.6 4.4 %collective-permute-start.2 = (bf16[1,47,128]{2,0,1:T(2,128)(2,1)S(1)}, bf16[1,47,128]{2,0,1:T(2,128)(2,1)S(1)}, u32[]{:S(2)}, u32[]{:S(2)}) collective-permute-start(bf16[1,47,128]{2,0,1:T(2,128)(2,1)S(1)} %get-tuple-element.8), channel_id=1, source_target_pairs={{0,32},{32,64},{64,96},{1,33},{33,65},{65,97},{2,34},{34,66},{66,9... | collective-permute-start | bytes 36104 | tf_op jit(solution)/shard_map/ppermute | solution.py:17
  21.7 4.6 %collective-permute-start.3 = (bf16[1,47,128]{2,0,1:T(2,128)(2,1)S(1)}, bf16[1,47,128]{2,0,1:T(2,128)(2,1)S(1)}, u32[]{:S(2)}, u32[]{:S(2)}) collective-permute-start(bf16[1,47,128]{2,0,1:T(2,128)(2,1)S(1)} %get-tuple-element.9), channel_id=1, source_target_pairs={{32,0},{64,32},{96,64},{33,1},{65,33},{97,65},{34,2},{66,34},{98,6... | collective-permute-start | bytes 36104 | tf_op jit(solution)/shard_map/ppermute | solution.py:20
  27.5 0.8 copy-start.10
  45.7 38.6 %collective-permute-start.4 = (bf16[180,45,80]{0,2,1:T(8,128)(2,1)}, bf16[180,45,80]{0,2,1:T(8,128)(2,1)}, u32[]{:S(2)}, u32[]{:S(2)}) collective-permute-start(bf16[180,45,80]{0,2,1:T(8,128)(2,1)} %bitcast.6), channel_id=1, source_target_pairs={{0,128},{128,0},{1,129},{129,1},{2,130},{130,2},{3,131},{131,3},{4... | collective-permute-start | bytes 3888008 | tf_op jit(solution)/shard_map/ppermute | solution.py:28
  53.4 31.0 %copy-start.5 = (bf16[180,45,80]{0,2,1:T(8,128)(2,1)S(1)}, bf16[180,45,80]{0,2,1:T(8,128)(2,1)}, u32[]{:S(2)}) copy-start(bf16[180,45,80]{0,2,1:T(8,128)(2,1)} %param.6) | copy-start | bytes 3888004
  98.1 3.0 copy-start.2
  98.1 3.4 copy-start.7
  102.2 1.6 copy-start.6
  112.0 8.4 %copy-start.3 = (bf16[180,45,80]{0,2,1:T(8,128)(2,1)S(1)}, bf16[180,45,80]{0,2,1:T(8,128)(2,1)}, u32[]{:S(2)}) copy-start(bf16[180,45,80]{0,2,1:T(8,128)(2,1)} %multiply_convert_fusion) | copy-start | bytes 3888004
  112.0 10.1 %collective-permute-start.5 = (bf16[180,1,80]{0,2,1:T(8,128)(2,1)S(1)}, bf16[180,1,80]{0,2,1:T(8,128)(2,1)S(1)}, u32[]{:S(2)}, u32[]{:S(2)}) collective-permute-start(bf16[180,1,80]{0,2,1:T(8,128)(2,1)S(1)} %get-tuple-element.14), channel_id=1, source_target_pairs={{0,1},{1,2},{2,3},{3,4},{4,5},{5,6},{6,7},{7,8},{8,9},{9,10},{10,1... | collective-permute-start | bytes 86408 | tf_op jit(solution)/shard_map/ppermute | solution.py:17
  117.5 4.9 %collective-permute-start.6 = (bf16[180,1,80]{0,2,1:T(8,128)(2,1)S(1)}, bf16[180,1,80]{0,2,1:T(8,128)(2,1)S(1)}, u32[]{:S(2)}, u32[]{:S(2)}) collective-permute-start(bf16[180,1,80]{0,2,1:T(8,128)(2,1)S(1)} %get-tuple-element.15), channel_id=1, source_target_pairs={{1,0},{2,1},{3,2},{4,3},{5,4},{6,5},{7,6},{8,7},{9,8},{10,9},{11,1... | collective-permute-start | bytes 86408 | tf_op jit(solution)/shard_map/ppermute | solution.py:20
  122.4 0.6 copy-start.8
  126.4 90.0 %copy-start.4 = (bf16[180,45,80]{0,2,1:T(8,128)(2,1)S(1)}, bf16[180,45,80]{0,2,1:T(8,128)(2,1)}, u32[]{:S(2)}) copy-start(bf16[180,45,80]{0,2,1:T(8,128)(2,1)} %multiply_convert_fusion) | copy-start | bytes 3888004
  126.4 90.0 %copy-start.9 = (bf16[180,1,80]{0,2,1:T(8,128)(2,1)S(1)}, bf16[180,1,80]{0,2,1:T(8,128)(2,1)}, u32[]{:S(2)}) copy-start(bf16[180,1,80]{0,2,1:T(8,128)(2,1)} %copy-done.8) | copy-start | bytes 86404
  126.4 88.1 %collective-permute-start.7 = (bf16[1,47,80]{2,1,0:T(8,128)(2,1)S(1)}, bf16[1,47,80]{2,1,0:T(8,128)(2,1)S(1)}, u32[]{:S(2)}, u32[]{:S(2)}) collective-permute-start(bf16[1,47,80]{2,1,0:T(8,128)(2,1)S(1)} %copy.19), channel_id=1, source_target_pairs={{0,32},{32,64},{64,96},{1,33},{33,65},{65,97},{2,34},{34,66},{66,9... | collective-permute-start | bytes 22568 | tf_op jit(solution)/shard_map/ppermute | solution.py:17
  130.1 84.9 %collective-permute-start.8 = (bf16[1,47,80]{2,1,0:T(8,128)(2,1)S(1)}, bf16[1,47,80]{2,1,0:T(8,128)(2,1)S(1)}, u32[]{:S(2)}, u32[]{:S(2)}) collective-permute-start(bf16[1,47,80]{2,1,0:T(8,128)(2,1)S(1)} %copy.20), channel_id=1, source_target_pairs={{32,0},{64,32},{96,64},{33,1},{65,33},{97,65},{34,2},{66,34},{98,6... | collective-permute-start | bytes 22568 | tf_op jit(solution)/shard_map/ppermute | solution.py:20
  219.1 4.7 %copy-start.11 = (pred[8,6]{0,1:T(8,128)(4,1)S(1)}, pred[8,6]{0,1:T(8,128)(4,1)}, u32[]{:S(2)}) copy-start(pred[8,6]{0,1:T(8,128)(4,1)} %constant.45) | copy-start | bytes 148
Sparse Core Ops, SparseCore 0:
  132.3 252.8 all-reduce.1
where the time goes:
time: 403 us; the launch traced here: 395 us
  waiting for transfers between devices  187 us (46%)
  blocking collectives  81.6 us (20%)
  local copies, waits for them, and re-layouts  37.2 us (9%)
  matrix products  26.9 us (7%)
  other arithmetic  25.9 us (6%)
  starting transfers between devices  19.2 us (5%)
  between operations  17.1 us (4%)
    psum x1, waiting for transfers between devices, local(): lax.psum((partial_grad, local_total), ('member', 'lat', 'lon'))  152 us
    psum x1, blocking collectives, local(): lax.psum((partial_grad, local_total), ('member', 'lat', 'lon'))  81.6 us
    ppermute x1, waiting for transfers between devices, partner(): return lax.ppermute(value, axis, pairs)  26.6 us
    ppermute x4, starting transfers between devices, padded(): lax.ppermute(lax.slice_in_dim(block, block.shape[dim] - width, None, axis...  16.2 us
    conv_general_dilated x2, matrix products, stencil_filter_step(): lax.conv_general_dilated(haloed_grid_array[None], weights_hwio, (1, 1), '...  14 us
    dot_general x9, matrix products, tap_products(): lax.dot_general(window, flat_grad, (((0,), (0,)), ((), ())), preferred_el...  12.9 us
    conv_general_dilated x5, local copies, waits for them, and re-layouts, stencil_filter_step(): lax.conv_general_dilated(haloed_grid_array[None], weights_hwio, (1, 1), '...  11.6 us
  transfers between devices with their start and end apart: 10, of which 6 were waited for; matrix products, arithmetic and copies ran while one was open for 9% of the time, Pallas kernels for 0%

commit v1 on v0

--- a/solution.py
+++ b/solution.py
@@ -107,7 +107,8 @@
         jnp.bfloat16
     )
     partial_grad = tap_products(haloed_grid_array, cotangent)
-    summed_grad, total = lax.psum((partial_grad, local_total), ("member", "lat", "lon"))
+    samples_mark = lambda state: lax.psum(lax.psum(state, ("lat", "lon")), "member")
+    summed_grad, total = samples_mark((partial_grad, local_total))
     objective_mean = total / (total_rows * total_cols)
     filter_weights_slope = summed_grad / math.sqrt(2.0 * total_rows * total_cols)
     return (predicted_outputs[None], objective_mean, hidden_state_slope[None], filter_weights_slope)

time: 403 us -> 1330 us (3.30)
  waiting for transfers between devices: 187 us -> 862 us
  blocking collectives: 81.6 us -> 334 us
    psum x1 -> x2, waiting for transfers between devices: 152 us -> 828 us  [the longest x1 802 us: local(): lax.psum(state, ('lat', 'lon'))]
    psum x1 -> x2, blocking collectives: 81.6 us -> 334 us  [the longest x1 329 us: local(): lax.psum(state, ('lat', 'lon'))]
  transfers between devices with their start and end apart: 10 -> 11, of which waited for: 6 -> 6; matrix products, arithmetic and copies ran while one was open for 9% -> 3% of each run, Pallas kernels for 0% -> 0%
where the time goes in v1:
time: 1330 us; the launch traced here: 1320 us
  waiting for transfers between devices  862 us (65%)
  blocking collectives  334 us (25%)
  local copies, waits for them, and re-layouts  37.1 us (3%)
  other arithmetic  27.4 us (2%)
  matrix products  27 us (2%)
  starting transfers between devices  19.2 us (1%)
  between operations  17 us (1%)
    psum x1, waiting for transfers between devices, local(): lax.psum(state, ('lat', 'lon'))  802 us
    psum x1, blocking collectives, local(): lax.psum(state, ('lat', 'lon'))  329 us
  transfers between devices with their start and end apart: 11, of which 6 were waited for; matrix products, arithmetic and copies ran while one was open for 3% of the time, Pallas kernels for 0%

profile of v1, /device:TPU:1, one launch (start us, length us, event | category | flops | bytes accessed | tf_op | source)
XLA Modules:
  0.0 1323.7 jit_solution(8460079494731881473)
XLA Ops:
  7.2 1.0 fusion.76
  8.2 4.4 collective-permute-start
  12.6 1.2 collective-permute-done
  13.7 3.8 collective-permute-done.1
  17.6 1.0 pad_maximum_fusion.5
  18.6 3.1 collective-permute-start.2
  21.7 1.3 collective-permute-start.3
  23.0 3.3 collective-permute-done.3
  26.3 1.0 maximum_bitcast_fusion
  28.3 6.8 broadcast_select_fusion
  35.1 6.2 copy.18
  41.3 4.4 fusion.3
  46.1 1.7 copy.27
  47.8 4.5 reshape_squeeze.3
  53.7 4.4 maximum_maximum_fusion
  58.0 26.3 %collective-permute-done.4 = bf16[180,45,80]{0,2,1:T(8,128)(2,1)} collective-permute-done((bf16[180,45,80]{0,2,1:T(8,128)(2,1)}, bf16[180,45,80]{0,2,1:T(8,128)(2,1)}, u32[]{:S(2)}, u32[]{:S(2)}) %collective-permute-start.4) | collective-permute-done | bytes 1296032 | tf_op jit(solution)/shard_map/ppermute | solution.py:28
  84.3 3.6 multiply_reduce_fusion
  88.6 4.8 multiply_convert_fusion
  93.4 4.7 copy.26
  98.1 3.0 fusion.44
  101.4 0.8 fusion.47
  102.2 0.8 fusion.50
  103.0 0.8 copy-done.6
  103.9 1.3 fusion.53
  105.1 1.3 fusion.56
  106.4 1.3 fusion.59
  107.7 4.2 reshape.50
  111.9 5.5 collective-permute-start.5
  117.4 3.1 convolution_bitcast_fusion
  120.5 0.8 fusion.62
  121.3 0.8 fusion.65
  122.2 0.8 pad_maximum_fusion.2
  123.0 1.9 pad_maximum_fusion.1
  124.9 1.4 fusion.77
  126.3 1.7 copy.19
  128.0 3.1 collective-permute-start.7
  131.6 1.3 collective-permute-start.8
  132.9 329.4 %psum.28 = f32[]{:T(128)} all-reduce(f32[]{:T(128)} %get-tuple-element.17), channel_id=1, replica_groups=mesh['member'=2,'lat'=4,'lon'=32] {'lat','lon'}, use_global_device_ids=true, to_apply=%region_4.0 | all-reduce | flops 1 | bytes 8 | tf_op jit(solution)/shard_map/psum | solution.py:110
  462.3 4.4 psum.29
  467.8 1.4 copy.22
  469.2 2.4 maximum_bitcast_fusion.1
  472.0 3.5 copy.24
  475.5 1.3 slice.84
  476.9 802.0 %all-reduce.3.cloned.1.call-done = f32[3,3,128,80]{2,3,1,0:T(8,128)} async-done(((f32[3,3,128,80]{2,3,1,0:T(8,128)}), f32[3,3,128,80]{2,3,1,0:T(8,128)}) %all-reduce.3.cloned.1.call-update) | async-done | bytes 368656 | tf_op jit(solution)/shard_map/psum | solution.py:110
  1278.8 7.1 select_convert_fusion
  1286.6 1.5 slice_bitcast_fusion.1
  1288.0 25.7 %all-reduce.5.cloned.1.call-done = f32[3,3,128,80]{2,3,1,0:T(8,128)} async-done(((f32[3,3,128,80]{2,3,1,0:T(8,128)}), f32[3,3,128,80]{2,3,1,0:T(8,128)}) %all-reduce.5.cloned.1.call-update) | async-done | bytes 368656 | tf_op jit(solution)/shard_map/psum | solution.py:110
  1313.8 1.8 broadcast_multiply_fusion
  (42 shorter events, 5.1 us)
Async XLA Ops:
  7.2 21.1 %copy-start = (bf16[3,3,128,80]{2,3,1,0:T(8,128)(2,1)S(1)}, bf16[3,3,128,80]{2,3,1,0:T(8,128)(2,1)}, u32[]{:S(2)}) copy-start(bf16[3,3,128,80]{2,3,1,0:T(8,128)(2,1)} %param.7) | copy-start | bytes 552964
  7.2 19.1 %copy-start.1 = (bf16[1,180,45,128]{3,1,2,0:T(8,128)(2,1)S(1)}, bf16[1,180,45,128]{3,1,2,0:T(8,128)(2,1)}, u32[]{:S(2)}) copy-start(bf16[1,180,45,128]{3,1,2,0:T(8,128)(2,1)} %param.4) | copy-start | bytes 6220804
  7.2 1271.6 %all-reduce.3.cloned.1.call-start = ((), (), s32[]{:S(2)}) async-start(), calls=%async_computation | async-start | bytes 737280 | tf_op jit(solution)/shard_map/psum | solution.py:110
  8.2 5.5 collective-permute-start
  12.6 5.0 collective-permute-start.1
  18.6 4.4 collective-permute-start.2
  21.7 4.6 collective-permute-start.3
  27.5 0.8 copy-start.8
  45.7 38.6 %collective-permute-start.4 = (bf16[180,45,80]{0,2,1:T(8,128)(2,1)}, bf16[180,45,80]{0,2,1:T(8,128)(2,1)}, u32[]{:S(2)}, u32[]{:S(2)}) collective-permute-start(bf16[180,45,80]{0,2,1:T(8,128)(2,1)} %bitcast.6), channel_id=1, source_target_pairs={{0,128},{128,0},{1,129},{129,1},{2,130},{130,2},{3,131},{131,3},{4... | collective-permute-start | bytes 3888008 | tf_op jit(solution)/shard_map/ppermute | solution.py:28
  53.7 30.7 %copy-start.5 = (bf16[180,45,80]{0,2,1:T(8,128)(2,1)S(1)}, bf16[180,45,80]{0,2,1:T(8,128)(2,1)}, u32[]{:S(2)}) copy-start(bf16[180,45,80]{0,2,1:T(8,128)(2,1)} %param.6) | copy-start | bytes 3888004
  98.1 3.0 copy-start.2
  98.1 3.4 copy-start.7
  102.2 1.6 copy-start.6
  111.9 11.1 collective-permute-start.5
  117.4 3.1 copy-start.3
  117.4 5.6 collective-permute-start.6
  123.0 1190.8 %all-reduce.5.cloned.1.call-start = ((), (), s32[]{:S(2)}) async-start(), calls=%async_computation.1 | async-start | bytes 737280 | tf_op jit(solution)/shard_map/psum | solution.py:110
  126.3 342.9 %copy-start.4 = (bf16[180,45,80]{0,2,1:T(8,128)(2,1)S(1)}, bf16[180,45,80]{0,2,1:T(8,128)(2,1)}, u32[]{:S(2)}) copy-start(bf16[180,45,80]{0,2,1:T(8,128)(2,1)} %multiply_convert_fusion) | copy-start | bytes 3888004
  128.0 339.3 %collective-permute-start.7 = (bf16[1,47,80]{2,1,0:T(8,128)(2,1)S(1)}, bf16[1,47,80]{2,1,0:T(8,128)(2,1)S(1)}, u32[]{:S(2)}, u32[]{:S(2)}) collective-permute-start(bf16[1,47,80]{2,1,0:T(8,128)(2,1)S(1)} %copy.19), channel_id=1, source_target_pairs={{0,32},{32,64},{64,96},{1,33},{33,65},{65,97},{2,34},{34,66},{66,9... | collective-permute-start | bytes 22568 | tf_op jit(solution)/shard_map/ppermute | solution.py:17
  131.6 336.2 %collective-permute-start.8 = (bf16[1,47,80]{2,1,0:T(8,128)(2,1)S(1)}, bf16[1,47,80]{2,1,0:T(8,128)(2,1)S(1)}, u32[]{:S(2)}, u32[]{:S(2)}) collective-permute-start(bf16[1,47,80]{2,1,0:T(8,128)(2,1)S(1)} %copy.20), channel_id=1, source_target_pairs={{32,0},{64,32},{96,64},{33,1},{65,33},{97,65},{34,2},{66,34},{98,6... | collective-permute-start | bytes 22568 | tf_op jit(solution)/shard_map/ppermute | solution.py:20
Sparse Core Ops, SparseCore 0:
  123.1 1155.6 all-reduce.2
  1281.6 32.1 all-reduce.4
